TPU v7x, 32 devices: a whole 2x2x4 slice. The times are simulated.
32 devices in a mesh: seq: 8 (over z, x), head: 4 (over y, core).
Axes of the slice: x: 2, y: 2, z: 4, core: 2. Of those that a mesh axis runs over, the one named last changes fastest.
Arguments:
- queries: bfloat16 [8192, 2048], P('seq', 'head'), may hold values from -100 to 100
- keys: bfloat16 [8192, 2048], P('seq', 'head'), may hold values from -8 to 8
- values: bfloat16 [8192, 2048], P('seq', 'head'), may hold values from -6 to 6
- rates: float32 [8192, 8], P('seq', 'head'), may hold values from 0.001 to 0.01
- head_scale: float32 [8], P('head'), may hold values from 0.3 to 3
- w_one: float32 [8, 256, 256], P('head'), may hold values from -0.375 to 0.375
- w_three: float32 [8, 256, 256], P('head'), may hold values from -0.375 to 0.375
- w_two: float32 [8, 256, 256], P('head'), may hold values from -0.375 to 0.375
Outputs:
- mixed: float32 [8192, 2048], P('seq', 'head')
- new_one: float32 [8, 256, 256], P('head')
- new_three: float32 [8, 256, 256], P('head')
- new_two: float32 [8, 256, 256], P('head')
All inputs are finite; a program needn't handle non-finite values.
Results may differ from a plain program's by a relative error of at most 0.00065.
Values may be sent and summed in bfloat16 or wider, within the bound.
No kernel may reach another device: no remote copies, remote signals or barrier semaphores. Data moves between devices by JAX's collectives and lax.ppermute only.
A program may use at most 64 MiB of HBM per device.

v0:
```python
import jax
import jax.numpy as jnp
from jax import lax
from jax.sharding import PartitionSpec as P

WINDOW_SPAN = 512
HIGH = lax.Precision.HIGHEST
EPS = 1e-06


def passed_along(block, axis, distance):
    devices = range(lax.axis_size(axis))
    route = [(i - distance, i) for i in devices if i - distance in devices]
    return lax.ppermute(block, axis, route)


def renorm(weight, grad):
    upd = weight + grad
    old = jnp.sqrt(jnp.sum(weight * weight, axis=2, keepdims=True) + EPS)
    cur = jnp.sqrt(jnp.sum(upd * upd, axis=2, keepdims=True) + EPS)
    return upd * (old / cur)


def per_device(queries, keys, values, rates, head_scale, w_one, w_three, w_two):
    tokens, width = queries.shape
    head_group = w_one.shape[0]
    span_size = w_one.shape[1]
    kf = keys.reshape(tokens, head_group, span_size).astype(jnp.float32)
    vf = values.reshape(tokens, head_group, span_size).astype(jnp.float32)
    h1 = jnp.einsum("thi,hij->thj", kf, w_one, precision=HIGH)
    h3 = jnp.einsum("thi,hij->thj", kf, w_three, precision=HIGH)
    sg = jax.nn.sigmoid(h1)
    sil = h1 * sg
    act = sil * h3
    scaled = rates[:, :, None] * vf
    g2 = jnp.einsum("thi,thj->hij", act, scaled, precision=HIGH)
    dact = jnp.einsum("thj,hij->thi", scaled, w_two, precision=HIGH)
    d1 = dact * h3 * sg * (1.0 + h1 * (1.0 - sg))
    d3 = dact * sil
    g1 = jnp.einsum("thi,thj->hij", kf, d1, precision=HIGH)
    g3 = jnp.einsum("thi,thj->hij", kf, d3, precision=HIGH)
    grads = jnp.stack([g1, g3, g2])
    weights = jnp.stack([w_one, w_three, w_two])
    summed = lax.psum(grads, "seq")
    updated = renorm(weights, summed)
    qf = queries.reshape(tokens, head_group, span_size).astype(jnp.float32)
    p1 = jnp.einsum("thi,hij->thj", qf, updated[0], precision=HIGH)
    p3 = jnp.einsum("thi,hij->thj", qf, updated[1], precision=HIGH)
    outer = jnp.einsum("thi,hij->thj", p1 * jax.nn.sigmoid(p1) * p3, updated[2], precision=HIGH)
    zed = outer * head_scale[None, :, None]
    local_sq = jnp.sum(zed * zed, axis=(1, 2))
    total_sq = lax.psum(local_sq, "head")
    all_heads = head_group * lax.axis_size("head")
    ynorm = zed / jnp.sqrt(total_sq / (all_heads * span_size) + EPS)[:, None, None]
    prior_keys, prior_values = passed_along(
        (keys[tokens - WINDOW_SPAN :], values[tokens - WINDOW_SPAN :]), "seq", 1
    )
    ext_keys = jnp.concatenate([prior_keys, keys], axis=0)
    ext_values = jnp.concatenate([prior_values, values], axis=0)
    offset = lax.axis_index("seq") * tokens
    block_span = min(512, tokens)
    scale = span_size ** (-0.5)
    query_rows = queries.reshape(tokens, head_group, span_size)
    rows = jnp.arange(block_span, dtype=jnp.int32)[:, None]
    cols = jnp.arange(block_span + WINDOW_SPAN, dtype=jnp.int32)[None, :]
    outputs = []
    for index in range(tokens // block_span):
        start_offset = index * block_span
        qb = query_rows[start_offset : start_offset + block_span]
        kb = ext_keys[start_offset : start_offset + block_span + WINDOW_SPAN].reshape(
            block_span + WINDOW_SPAN, head_group, span_size
        )
        value_block = ext_values[start_offset : start_offset + block_span + WINDOW_SPAN].reshape(
            block_span + WINDOW_SPAN, head_group, span_size
        )
        scores = jnp.einsum("ihd,jhd->hij", qb, kb, preferred_element_type=jnp.float32) * scale
        allowed = (
            (cols > rows)
            & (cols <= rows + WINDOW_SPAN)
            & (offset + start_offset + cols - WINDOW_SPAN >= 0)
        )
        scores = jnp.where(allowed[None], scores, -jnp.inf)
        top = jnp.max(scores, axis=-1, keepdims=True)
        expo = jnp.exp(scores - top)
        probs = (expo / jnp.sum(expo, axis=-1, keepdims=True)).astype(jnp.bfloat16)
        outputs.append(
            jnp.einsum("hij,jhd->ihd", probs, value_block, preferred_element_type=jnp.float32)
        )
    attn = jnp.concatenate(outputs, axis=0)
    mixed = (attn + ynorm).reshape(tokens, width)
    return (mixed, updated[0], updated[1], updated[2])


def solution(mesh):
    placed = (
        P("seq", "head"),
        P("seq", "head"),
        P("seq", "head"),
        P("seq", "head"),
        P("head"),
        P("head", None, None),
        P("head", None, None),
        P("head", None, None),
    )
    return jax.shard_map(
        per_device,
        mesh=mesh,
        in_specs=placed,
        out_specs=(
            P("seq", "head"),
            P("head", None, None),
            P("head", None, None),
            P("head", None, None),
        ),
        check_vma=False,
    )
```

profile of v0, /device:TPU:0, one launch (start us, length us, event | category | flops | bytes accessed | tf_op | source)
XLA Modules:
  0.0 156.2 jit_solution(4085122820597127520)
XLA Ops:
  7.2 0.0 copy-start
  7.2 0.0 copy-start.7
  7.2 0.0 all-reduce.2.cloned.1.call-start
  7.2 2.0 %slice.36 = bf16[512,512]{1,0:T(8,128)(2,1)} slice(bf16[1024,512]{1,0:T(8,128)(2,1)} %param.10), slice={[512:1024], [0:512]} | slice | bytes 1048576 | tf_op jit(solution)/shard_map/slice | solution.py:56
  9.2 5.7 %collective-permute-start = (bf16[512,512]{1,0:T(8,128)(2,1)}, bf16[512,512]{1,0:T(8,128)(2,1)}, u32[]{:S(2)}, u32[]{:S(2)}) collective-permute-start(bf16[512,512]{1,0:T(8,128)(2,1)} %slice.36), channel_id=1, source_target_pairs={{0,4},{4,8},{8,12},{12,16},{16,20},{20,24},{24,28},{1,5},{5,9},{9,... | collective-permute-start | bytes 1572872 | tf_op jit(solution)/shard_map/ppermute | solution.py:14
  14.9 1.5 copy.42
  16.4 0.8 slice.47
  17.2 0.0 copy-start.8
  17.2 3.6 %collective-permute-start.1 = (bf16[512,512]{0,1:T(8,128)(2,1)}, bf16[512,512]{0,1:T(8,128)(2,1)}, u32[]{:S(2)}, u32[]{:S(2)}) collective-permute-start(bf16[512,512]{0,1:T(8,128)(2,1)} %slice.47), channel_id=1, source_target_pairs={{0,4},{4,8},{8,12},{12,16},{16,20},{20,24},{24,28},{1,5},{5,9},{9,... | collective-permute-start | bytes 1572872 | tf_op jit(solution)/shard_map/ppermute | solution.py:14
  20.8 0.0 copy-done
  20.8 0.0 copy-done.7
  20.8 1.1 fusion.49
  21.9 0.0 copy-done.8
  21.9 0.0 copy-start.1
  21.9 0.0 copy-start.6
  21.9 0.0 copy-start.9
  21.9 1.1 fusion.47
  23.0 0.1 copy-done.1
  23.1 0.1 copy-done.6
  23.3 0.0 copy-done.9
  23.3 2.1 %fusion.22 = f32[2,1024,256]{2,1,0:T(8,128)S(1)} fusion(f32[2,256,256]{2,1,0:T(8,128)S(1)} %copy-done.6, f32[1024,2]{0,1:T(2,128)S(1)} %copy-done.9, bf16[128,2,8,256]{3,2,1,0:T(8,128)(2,1)S(1)} %bitcast.165), kind=kOutput, calls=%fused_computation.37 | convolution fusion | flops 1611661312 | bytes 3678208 | tf_op jit(solution)/shard_map/thj,hij->thi/dot_general | solution.py:37
  25.3 4.2 %fusion.39 = f32[1,2,256,256]{2,3,1,0:T(8,128)S(1)} fusion(f32[2,256,1024]{1,2,0:T(8,128)S(1)} %fusion.49, f32[1024,2]{0,1:T(2,128)S(1)} %copy-done.9, bf16[128,2,8,256]{3,2,1,0:T(8,128)(2,1)S(1)} %bitcast.166, f32[2,256,1024]{1,2,0:T(8,128)S(1)} %fusion.47), kind=kOutput, calls=%fused_computation.58 | convolution fusion | flops 1614282752 | bytes 5775360 | tf_op jit(solution)/shard_map/thi,thj->hij/dot_general | solution.py:36
  29.6 2.0 %fusion.40 = f32[1,2,256,256]{2,3,1,0:T(8,128)S(1)} fusion(f32[2,1024,256]{2,1,0:T(8,128)S(1)} %fusion.22, bf16[128,2,8,256]{3,2,1,0:T(8,128)(2,1)S(1)} %bitcast.159, f32[2,256,1024]{1,2,0:T(8,128)S(1)} %fusion.47), kind=kOutput, calls=%fused_computation.59 | convolution fusion | flops 1613234176 | bytes 5767168 | tf_op jit(solution)/shard_map/thi,thj->hij/dot_general | solution.py:41
  31.6 2.5 %fusion.36 = f32[1,2,256,256]{2,3,1,0:T(8,128)S(1)} fusion(f32[2,256,1024]{1,2,0:T(8,128)S(1)} %fusion.47, f32[2,256,1024]{1,2,0:T(8,128)S(1)} %fusion.49, f32[2,1024,256]{2,1,0:T(8,128)S(1)} %fusion.22, bf16[128,2,8,256]{3,2,1,0:T(8,128)(2,1)S(1)} %bitcast.160), kind=kOutput, calls=%fused_computation.57 | convolution fusion | flops 1615331328 | bytes 7864320 | tf_op jit(solution)/shard_map/thi,thj->hij/dot_general | solution.py:40
  34.1 1.2 pad_maximum_fusion.1
  35.3 0.0 all-reduce.2.cloned.1.call-update
  35.4 2.2 %fusion.77 = (bf16[512,512]{1,0:T(8,128)(2,1)}, bf16[512,512]{1,0:T(8,128)(2,1)}) fusion(bf16[1024,512]{1,0:T(8,128)(2,1)} %param.8), kind=kLoop, calls=%fused_computation.106 | loop fusion | bytes 2097152 | tf_op jit(solution)/shard_map/slice | solution.py:69
  37.6 2.0 %copy.95 = bf16[512,512]{0,1:T(8,128)(2,1)} copy(bf16[512,512]{1,0:T(8,128)(2,1)} %get-tuple-element.18) | data formatting | bytes 1048576
  39.7 3.9 %fusion.51 = f32[2,512,1024]{1,2,0:T(8,128)} fusion(bf16[512,2,256]{0,2,1:T(8,128)(2,1)} %bitcast.174, bf16[128,2,8,256]{3,2,1,0:T(8,128)(2,1)S(1)} %bitcast.161), kind=kOutput, calls=%fused_computation.70 | convolution fusion | flops 536870912 | bytes 5767168 | tf_op jit(solution)/shard_map/ihd,jhd->hij/dot_general | solution.py:76
  43.6 1.7 %fusion.33 = (pred[512,1024]{0,1:T(8,128)(4,1)}, pred[512,1024]{0,1:T(8,128)(4,1)S(1)}) fusion(s32[512]{0:T(512)S(1)} %iota_add_fusion, pred[1024]{0:T(1024)(128)(4,1)S(1)} %get-tuple-element.28, pred[1024]{0:T(1024)(128)(4,1)S(1)} %get-tuple-element.27), kind=kLoop, calls=%fused_computation.50 | loop fusion | flops 2621440 | bytes 1052672 | tf_op jit(solution)/shard_map/and | solution.py:78
  45.3 5.7 %fusion.78 = (f32[2,512]{1,0:T(2,128)S(1)}, f32[2,512,1024]{1,2,0:T(8,128)S(1)}) fusion(f32[2,512,1024]{1,2,0:T(8,128)} %fusion.51, pred[512,1024]{0,1:T(8,128)(4,1)S(1)} %get-tuple-element.20), kind=kOutput, calls=%fused_computation.107 | output fusion | flops 6292479 | bytes 8916992 | tf_op jit(solution)/shard_map/sub | solution.py:84
  51.0 1.7 %fusion.34 = f32[512,2,256]{0,2,1:T(8,128)} fusion(f32[2,512,1024]{1,2,0:T(8,128)S(1)} %get-tuple-element.22, f32[2,512]{1,0:T(2,128)S(1)} %get-tuple-element.21, bf16[128,2,8,256]{3,2,1,0:T(8,128)(2,1)S(1)} %bitcast.167), kind=kOutput, calls=%fused_computation.55 | convolution fusion | flops 538968064 | bytes 6295552 | tf_op jit(solution)/shard_map/hij,jhd->ihd/dot_general | solution.py:87
  52.7 1.5 copy.96
  54.2 2.1 %copy.57 = f32[2,256,256]{1,2,0:T(8,128)} copy(f32[2,256,256]{2,1,0:T(8,128)} %param.15) | data formatting | bytes 1048576 | tf_op args[7]
  56.3 2.0 %copy.56 = f32[2,256,256]{1,2,0:T(8,128)} copy(f32[2,256,256]{2,1,0:T(8,128)} %param.14) | data formatting | bytes 1048576 | tf_op args[6]
  58.3 2.1 %copy.55 = f32[2,256,256]{1,2,0:T(8,128)} copy(f32[2,256,256]{2,1,0:T(8,128)} %param.13) | data formatting | bytes 1048576 | tf_op args[5]
  60.4 2.1 %copy.94 = bf16[512,512]{0,1:T(8,128)(2,1)} copy(bf16[512,512]{1,0:T(8,128)(2,1)} %get-tuple-element.17) | data formatting | bytes 1048576
  62.4 0.0 collective-permute-done
  62.4 2.1 %pad_maximum_fusion.3 = bf16[1024,512]{1,0:T(8,128)(2,1)} fusion(bf16[1024,512]{1,0:T(8,128)(2,1)S(1)} %copy-done.1, bf16[512,512]{1,0:T(8,128)(2,1)} %collective-permute-done), kind=kLoop, calls=%fused_computation.73 | loop fusion | flops 2097152 | bytes 2621440 | tf_op jit(solution)/shard_map/concatenate | solution.py:59
  64.5 2.3 %copy.41 = bf16[1024,512]{0,1:T(8,128)(2,1)} copy(bf16[1024,512]{1,0:T(8,128)(2,1)} %pad_maximum_fusion.3) | data formatting | bytes 2097152 | tf_op jit(solution)/shard_map/slice | solution.py:73
  66.8 0.0 collective-permute-done.1
  66.8 1.1 pad_maximum_fusion.2
  68.0 5.0 %fusion.79 = (f32[2,512]{1,0:T(2,128)S(1)}, f32[2,512,1024]{1,2,0:T(8,128)}) fusion(pred[512,1024]{0,1:T(8,128)(4,1)} %get-tuple-element.19, bf16[1024,2,256]{0,2,1:T(8,128)(2,1)S(1)} %bitcast.176, bf16[512,2,256]{0,2,1:T(8,128)(2,1)} %bitcast.177), kind=kOutput, calls=%fused_computation.108 | convolution fusion | flops 541066240 | bytes 6295552 | tf_op jit(solution)/shard_map/sub | solution.py:84
  73.0 0.0 copy-start.4
  73.0 4.4 %fusion.35 = f32[512,2,256]{0,2,1:T(8,128)} fusion(bf16[1024,2,256]{0,2,1:T(8,128)(2,1)} %bitcast.175, f32[2,512,1024]{1,2,0:T(8,128)} %get-tuple-element.24, f32[2,512]{1,0:T(2,128)S(1)} %get-tuple-element.23), kind=kOutput, calls=%fused_computation.56 | convolution fusion | flops 538968064 | bytes 6295552 | tf_op jit(solution)/shard_map/hij,jhd->ihd/dot_general | solution.py:87
  77.4 46.9 %all-reduce.2.cloned.1.call-done = f32[3,2,256,256]{2,3,1,0:T(8,128)} async-done(((f32[3,2,256,256]{2,3,1,0:T(8,128)}), f32[3,2,256,256]{2,3,1,0:T(8,128)}) %all-reduce.2.cloned.1.call-update) | async-done | bytes 1572880 | tf_op jit(solution)/shard_map/psum | solution.py:44
  124.3 0.0 copy-done.3
  124.3 0.0 copy-done.4
  124.3 0.0 copy-done.5
  124.3 2.0 %multiply_reduce_fusion.2 = (f32[3,2,256]{2,1,0:T(2,128)S(1)}, f32[3,2,256]{2,1,0:T(2,128)S(1)}) fusion(f32[1,2,256,256]{2,3,1,0:T(8,128)S(1)} %bitcast.168, f32[1,2,256,256]{2,3,1,0:T(8,128)S(1)} %bitcast.170, f32[1,2,256,256]{2,3,1,0:T(8,128)S(1)} %bitcast.172, f32[3,2,256,256]{2,3,1,0:T(8,128)} %all-reduce.2.cloned.1.call-done), kind=kLoop, calls=%fused_computation.54 | loop fusion | flops 2749440 | bytes 3158016 | tf_op jit(solution)/shard_map/reduce_sum | solution.py:19
  126.3 0.0 copy-done.2
  126.3 0.4 broadcast_multiply_fusion
  126.7 1.2 fusion.76
  128.0 1.2 fusion.75
  129.2 0.0 copy-start.10
  129.2 1.0 slice_bitcast_fusion.2
  130.2 0.0 copy-done.10
  130.2 3.8 %multiply_reduce_fusion = (f32[1024]{0:T(1024)S(1)}, f32[2,256,1024]{2,1,0:T(8,128)}) fusion(f32[2]{0:T(128)S(1)} %copy-done.10, f32[2,256,1024]{1,2,0:T(8,128)S(1)} %fusion.76, f32[2,256,1024]{1,2,0:T(8,128)S(1)} %fusion.75, f32[3,2,256,256]{2,3,1,0:T(8,128)S(1)} %broadcast_multiply_fusion), kind=kOutput, calls=%fused_computation.34 | convolution fusion | flops 1614806016 | bytes 6820352 | tf_op jit(solution)/shard_map/thi,hij->thj/dot_general | solution.py:49
  134.0 6.8 %psum.15 = f32[1024]{0:T(1024)S(1)} all-reduce(f32[1024]{0:T(1024)S(1)} %get-tuple-element.25), channel_id=1, replica_groups=mesh['seq'=8,'head'=4] {'head'}, use_global_device_ids=true, to_apply=%region_8.9 | all-reduce | flops 1024 | bytes 8192 | tf_op jit(solution)/shard_map/psum | solution.py:52
  140.8 2.7 %maximum_add_fusion = f32[1024,2,256]{0,2,1:T(8,128)S(1)} fusion(f32[512,2,256]{0,2,1:T(8,128)} %fusion.34, f32[512,2,256]{0,2,1:T(8,128)} %fusion.35, f32[2,256,1024]{2,1,0:T(8,128)} %get-tuple-element.26, f32[1024]{0:T(1024)S(1)} %add_sqrt_fusion, f32[2]{0:T(128)S(1)} %copy-done.10), kind=kLoop, calls=%fused_computation.10 | loop fusion | flops 2097152 | bytes 6295560 | tf_op jit(solution)/shard_map/add | solution.py:90
  143.6 1.8 %copy.73 = f32[1024,512]{1,0:T(8,128)} copy(f32[1024,512]{0,1:T(8,128)S(1)} %bitcast.164) | data formatting | bytes 4194304
  145.4 2.0 %copy.74 = f32[2,256,256]{2,1,0:T(8,128)} copy(f32[2,256,256]{1,2,0:T(8,128)} %get-tuple-element.16) | data formatting | bytes 1048576
  147.4 1.0 copy.75
  148.4 1.0 copy.76
  (7 shorter events, 0.0 us)
Async XLA Ops:
  7.2 13.7 %copy-start = (bf16[1024,512]{1,0:T(8,128)(2,1)S(1)}, bf16[1024,512]{1,0:T(8,128)(2,1)}, u32[]{:S(2)}) copy-start(bf16[1024,512]{1,0:T(8,128)(2,1)} %param.9) | copy-start | bytes 3145732
  7.2 13.6 %copy-start.7 = (f32[2,256,256]{2,1,0:T(8,128)S(1)}, f32[2,256,256]{2,1,0:T(8,128)}, u32[]{:S(2)}) copy-start(f32[2,256,256]{2,1,0:T(8,128)} %param.14) | copy-start | bytes 1572868
  7.2 117.1 %all-reduce.2.cloned.1.call-start = ((), (), s32[]{:S(2)}) async-start(), calls=%async_computation | async-start | bytes 3145728 | tf_op jit(solution)/shard_map/psum | solution.py:44
  9.2 53.2 %collective-permute-start = (bf16[512,512]{1,0:T(8,128)(2,1)}, bf16[512,512]{1,0:T(8,128)(2,1)}, u32[]{:S(2)}, u32[]{:S(2)}) collective-permute-start(bf16[512,512]{1,0:T(8,128)(2,1)} %slice.36), channel_id=1, source_target_pairs={{0,4},{4,8},{8,12},{12,16},{16,20},{20,24},{24,28},{1,5},{5,9},{9,... | collective-permute-start | bytes 1572872 | tf_op jit(solution)/shard_map/ppermute | solution.py:14
  17.2 4.6 %copy-start.8 = (f32[2,256,256]{2,1,0:T(8,128)S(1)}, f32[2,256,256]{2,1,0:T(8,128)}, u32[]{:S(2)}) copy-start(f32[2,256,256]{2,1,0:T(8,128)} %param.13) | copy-start | bytes 1572868
  17.2 49.6 %collective-permute-start.1 = (bf16[512,512]{0,1:T(8,128)(2,1)}, bf16[512,512]{0,1:T(8,128)(2,1)}, u32[]{:S(2)}, u32[]{:S(2)}) collective-permute-start(bf16[512,512]{0,1:T(8,128)(2,1)} %slice.47), channel_id=1, source_target_pairs={{0,4},{4,8},{8,12},{12,16},{16,20},{20,24},{24,28},{1,5},{5,9},{9,... | collective-permute-start | bytes 1572872 | tf_op jit(solution)/shard_map/ppermute | solution.py:14
  21.9 1.2 copy-start.1
  21.9 1.3 copy-start.6
  21.9 1.3 copy-start.9
  73.0 51.3 %copy-start.3 = (f32[2,256,256]{1,2,0:T(8,128)S(1)}, f32[2,256,256]{1,2,0:T(8,128)}, u32[]{:S(2)}) copy-start(f32[2,256,256]{1,2,0:T(8,128)} %copy.57) | copy-start | bytes 1572868
  73.0 51.3 %copy-start.4 = (f32[2,256,256]{1,2,0:T(8,128)S(1)}, f32[2,256,256]{1,2,0:T(8,128)}, u32[]{:S(2)}) copy-start(f32[2,256,256]{1,2,0:T(8,128)} %copy.56) | copy-start | bytes 1572868
  73.0 51.3 %copy-start.5 = (f32[2,256,256]{1,2,0:T(8,128)S(1)}, f32[2,256,256]{1,2,0:T(8,128)}, u32[]{:S(2)}) copy-start(f32[2,256,256]{1,2,0:T(8,128)} %copy.55) | copy-start | bytes 1572868
  124.3 2.1 %copy-start.2 = (f32[3,2,256,256]{2,3,1,0:T(8,128)S(1)}, f32[3,2,256,256]{2,3,1,0:T(8,128)}, u32[]{:S(2)}) copy-start(f32[3,2,256,256]{2,3,1,0:T(8,128)} %all-reduce.2.cloned.1.call-done) | copy-start | bytes 4718596
  129.2 1.0 copy-start.10
Sparse Core Ops, SparseCore 0:
  35.5 88.7 all-reduce.1
where the time goes:
time: 157 us; the launch traced here: 156 us
  waiting for transfers between devices  46.9 us (30%)
  matrix products  34.3 us (22%)
  local copies, waits for them, and re-layouts  27.7 us (18%)
  other arithmetic  17 us (11%)
  between operations  14.2 us (9%)
  starting transfers between devices  9.28 us (6%)
  blocking collectives  6.81 us (4%)
    psum x1, waiting for transfers between devices, per_device(): summed = lax.psum(grads, 'seq')  46.9 us
    unnamed x32, local copies, waits for them, and re-layouts  17.9 us
    ppermute x2, starting transfers between devices, passed_along(): return lax.ppermute(block, axis, route)  9.25 us
    psum x1, blocking collectives, per_device(): total_sq = lax.psum(local_sq, 'head')  6.81 us
    dot_general x2, matrix products, per_device(): jnp.einsum('hij,jhd->ihd', probs, value_block, preferred_element_type=jnp...  6.11 us
    sub x1, other arithmetic, per_device(): expo = jnp.exp(scores - top)  5.66 us
    sub x1, matrix products, per_device(): expo = jnp.exp(scores - top)  5 us
    dot_general x1, matrix products, per_device(): g2 = jnp.einsum('thi,thj->hij', act, scaled, precision=HIGH)  4.22 us
  transfers between devices with their start and end apart: 3, of which 1 were waited for; matrix products, arithmetic and copies ran while one was open for 37% of the time, Pallas kernels for 0%

commit v1 on v0

--- a/solution.py
+++ b/solution.py
@@ -41,7 +41,9 @@
     g3 = jnp.einsum("thi,thj->hij", kf, d3, precision=HIGH)
     grads = jnp.stack([g1, g3, g2])
     weights = jnp.stack([w_one, w_three, w_two])
-    summed = lax.psum(grads, "seq")
+    summed = grads
+    for hop in (1, 2, 4):
+        summed = summed + lax.ppermute(summed, "seq", [(dev, dev ^ hop) for dev in range(8)])
     updated = renorm(weights, summed)
     qf = queries.reshape(tokens, head_group, span_size).astype(jnp.float32)
     p1 = jnp.einsum("thi,hij->thj", qf, updated[0], precision=HIGH)

time: 157 us -> 186 us (1.18)
  waiting for transfers between devices: 46.9 us -> 99.4 us
  local copies, waits for them, and re-layouts: 27.7 us -> 13.8 us
  between operations: 14.2 us -> 0.94 us
  starting transfers between devices: 9.28 us -> 13.8 us
    ppermute x0 -> x3, waiting for transfers between devices: none -> 99.4 us  [per_device(): lax.ppermute(summed, 'seq', [(dev, dev ^ hop) for dev in range(8)])]
    psum x1 -> x0, waiting for transfers between devices: 46.9 us -> none  [per_device(): summed = lax.psum(grads, 'seq')]
    unnamed x32 -> x48, local copies, waits for them, and re-layouts: 17.9 us -> 6.42 us
    ppermute x0 -> x3, starting transfers between devices: none -> 7.5 us  [per_device(): lax.ppermute(summed, 'seq', [(dev, dev ^ hop) for dev in range(8)])]
    sub x1 -> x0, other arithmetic: 5.66 us -> none  [per_device(): expo = jnp.exp(scores - top)]
    add x0 -> x2, other arithmetic: none -> 3.95 us  [per_device(): summed + lax.ppermute(summed, 'seq', [(dev, dev ^ hop) for dev in range(8)])]
    dot_general x1 -> x0, matrix products: 3.94 us -> none  [per_device(): jnp.einsum('ihd,jhd->hij', qb, kb, preferred_element_type=jnp.float32)]
    sub x1 -> x2, matrix products: 5 us -> 8.75 us  [per_device(): expo = jnp.exp(scores - top)]
  transfers between devices with their start and end apart: 3 -> 5, of which waited for: 1 -> 3; matrix products, arithmetic and copies ran while one was open for 37% -> 17% of each run, Pallas kernels for 0% -> 0%
where the time goes in v1:
time: 186 us; the launch traced here: 185 us
  waiting for transfers between devices  99.4 us (53%)
  matrix products  35.2 us (19%)
  other arithmetic  16.2 us (9%)
  local copies, waits for them, and re-layouts  13.8 us (7%)
  starting transfers between devices  13.8 us (7%)
  blocking collectives  5.63 us (3%)
    ppermute x3, waiting for transfers between devices, per_device(): lax.ppermute(summed, 'seq', [(dev, dev ^ hop) for dev in range(8)])  99.4 us
    sub x2, matrix products, per_device(): expo = jnp.exp(scores - top)  8.75 us
    ppermute x3, starting transfers between devices, per_device(): lax.ppermute(summed, 'seq', [(dev, dev ^ hop) for dev in range(8)])  7.5 us
    unnamed x48, local copies, waits for them, and re-layouts  6.42 us
    ppermute x2, starting transfers between devices, passed_along(): return lax.ppermute(block, axis, route)  6.33 us
    dot_general x2, matrix products, per_device(): jnp.einsum('hij,jhd->ihd', probs, value_block, preferred_element_type=jnp...  6.17 us
    psum x1, blocking collectives, per_device(): total_sq = lax.psum(local_sq, 'head')  5.63 us
    dot_general x1, matrix products, per_device(): jnp.einsum('thi,hij->thj', p1 * jax.nn.sigmoid(p1) * p3, updated[2], prec...  5.29 us
  transfers between devices with their start and end apart: 5, of which 3 were waited for; matrix products, arithmetic and copies ran while one was open for 17% of the time, Pallas kernels for 0%

profile of v1, /device:TPU:0, one launch (start us, length us, event | category | flops | bytes accessed | tf_op | source)
XLA Modules:
  0.0 185.0 jit_solution(927792076456634415)
XLA Ops:
  0.6 0.0 copy-start.8
  0.6 1.5 copy.35
  2.2 0.0 copy-start.10
  2.2 0.0 copy-done.8
  2.2 1.2 fusion.67
  3.4 0.0 copy-done.10
  3.5 0.0 copy-start.1
  3.5 0.0 copy-start.6
  3.5 0.0 copy-start.19
  3.5 1.2 fusion.68
  4.7 0.0 copy-done.1
  4.7 0.1 copy-done.6
  4.8 0.0 copy-done.19
  4.8 2.1 %fusion.22 = f32[2,1024,256]{2,1,0:T(8,128)S(1)} fusion(f32[2,256,256]{2,1,0:T(8,128)S(1)} %copy-done.6, f32[1024,2]{0,1:T(2,128)S(1)} %copy-done.19, bf16[128,2,8,256]{3,2,1,0:T(8,128)(2,1)S(1)} %bitcast.159), kind=kOutput, calls=%fused_computation.37 | convolution fusion | flops 1611661312 | bytes 3678208 | tf_op jit(solution)/shard_map/thj,hij->thi/dot_general | solution.py:37
  6.9 4.1 %fusion.39 = f32[1,2,256,256]{3,2,1,0:T(8,128)S(1)} fusion(f32[2,256,1024]{1,2,0:T(8,128)S(1)} %fusion.67, f32[1024,2]{0,1:T(2,128)S(1)} %copy-done.19, bf16[128,2,8,256]{3,2,1,0:T(8,128)(2,1)S(1)} %bitcast.160, f32[2,256,1024]{1,2,0:T(8,128)S(1)} %fusion.68), kind=kOutput, calls=%fused_computation.59 | convolution fusion | flops 1614282752 | bytes 5775360 | tf_op jit(solution)/shard_map/thi,thj->hij/dot_general | solution.py:36
  11.1 1.7 fusion.40
  12.8 0.0 copy-start.4
  12.8 2.1 %fusion.36 = f32[1,2,256,256]{3,2,1,0:T(8,128)S(1)} fusion(bf16[1024,2,256]{0,2,1:T(8,128)(2,1)S(1)} %bitcast.154, f32[2,256,1024]{1,2,0:T(8,128)S(1)} %fusion.68, f32[2,256,1024]{1,2,0:T(8,128)S(1)} %fusion.67, f32[2,1024,256]{2,1,0:T(8,128)S(1)} %fusion.22), kind=kOutput, calls=%fused_computation.58 | convolution fusion | flops 1615331328 | bytes 7864320 | tf_op jit(solution)/shard_map/thi,thj->hij/dot_general | solution.py:40
  14.9 0.0 copy-start.5
  14.9 0.1 pad_maximum_fusion.1
  15.1 3.0 %collective-permute-start.2 = (f32[3,2,256,256]{3,2,1,0:T(8,128)S(1)}, f32[3,2,256,256]{3,2,1,0:T(8,128)S(1)}, u32[]{:S(2)}, u32[]{:S(2)}) collective-permute-start(f32[3,2,256,256]{3,2,1,0:T(8,128)S(1)} %pad_maximum_fusion.1), channel_id=1, source_target_pairs={{0,4},{4,0},{8,12},{12,8},{16,20},{20,16},{24,28},{28,24},{1,5},{5... | collective-permute-start | bytes 4718600 | tf_op jit(solution)/shard_map/ppermute | solution.py:46
  18.1 34.4 %collective-permute-done.2 = f32[3,2,256,256]{3,2,1,0:T(8,128)S(1)} collective-permute-done((f32[3,2,256,256]{3,2,1,0:T(8,128)S(1)}, f32[3,2,256,256]{3,2,1,0:T(8,128)S(1)}, u32[]{:S(2)}, u32[]{:S(2)}) %collective-permute-start.2) | collective-permute-done | bytes 1572896 | tf_op jit(solution)/shard_map/ppermute | solution.py:46
  52.5 0.0 copy-done.4
  52.5 1.5 fusion.63
  54.0 0.0 copy-done.5
  54.0 0.2 copy-done.3
  54.2 1.8 collective-permute-start.3
  56.0 0.8 slice.36
  56.8 4.2 %collective-permute-start = (bf16[512,512]{1,0:T(8,128)(2,1)}, bf16[512,512]{1,0:T(8,128)(2,1)}, u32[]{:S(2)}, u32[]{:S(2)}) collective-permute-start(bf16[512,512]{1,0:T(8,128)(2,1)} %slice.36), channel_id=1, source_target_pairs={{0,4},{4,8},{8,12},{12,16},{16,20},{20,24},{24,28},{1,5},{5,9},{9,... | collective-permute-start | bytes 1572872 | tf_op jit(solution)/shard_map/ppermute | solution.py:14
  61.1 0.9 slice.47
  61.9 2.1 %collective-permute-start.1 = (bf16[512,512]{0,1:T(8,128)(2,1)}, bf16[512,512]{0,1:T(8,128)(2,1)}, u32[]{:S(2)}, u32[]{:S(2)}) collective-permute-start(bf16[512,512]{0,1:T(8,128)(2,1)} %slice.47), channel_id=1, source_target_pairs={{0,4},{4,8},{8,12},{12,16},{16,20},{20,24},{24,28},{1,5},{5,9},{9,... | collective-permute-start | bytes 1572872 | tf_op jit(solution)/shard_map/ppermute | solution.py:14
  64.1 0.0 copy-done.12
  64.1 0.9 fusion.64
  64.9 0.2 copy.80
  65.2 1.7 fusion.33
  66.9 3.7 %fusion.65 = (f32[2,512]{1,0:T(2,128)S(1)}, f32[2,512,1024]{1,2,0:T(8,128)}) fusion(pred[512,1024]{0,1:T(8,128)(4,1)S(1)} %get-tuple-element.20, bf16[1024,2,256]{0,2,1:T(8,128)(2,1)S(1)} %bitcast.155, bf16[512,2,256]{0,2,1:T(8,128)(2,1)S(1)} %bitcast.170), kind=kOutput, calls=%fused_computation.94 | convolution fusion | flops 541066240 | bytes 6295552 | tf_op jit(solution)/shard_map/sub | solution.py:86
  70.6 19.4 %collective-permute-done.3 = f32[3,2,256,256]{3,2,1,0:T(8,128)} collective-permute-done((f32[3,2,256,256]{3,2,1,0:T(8,128)}, f32[3,2,256,256]{3,2,1,0:T(8,128)}, u32[]{:S(2)}, u32[]{:S(2)}) %collective-permute-start.3) | collective-permute-done | bytes 1572896 | tf_op jit(solution)/shard_map/ppermute | solution.py:46
  90.0 2.5 %fusion.92 = f32[3,2,256,256]{3,2,1,0:T(8,128)S(1)} fusion(f32[3,2,256,256]{3,2,1,0:T(8,128)} %collective-permute-done.3, f32[3,2,256,256]{3,2,1,0:T(8,128)} %copy-done.3, f32[1,2,256,256]{3,2,1,0:T(8,128)S(1)} %fusion.39, f32[1,2,256,256]{3,2,1,0:T(8,128)} %copy-done.4, f32[1,2,256,256]{3,2,1,0:T(8,128)} %copy-done.5), kind=kLoop, calls=%fused_computation.100 | loop fusion | flops 1572864 | bytes 6291456 | tf_op jit(solution)/shard_map/add | solution.py:46
  92.5 2.6 %collective-permute-start.4 = (f32[3,2,256,256]{3,2,1,0:T(8,128)S(1)}, f32[3,2,256,256]{3,2,1,0:T(8,128)}, u32[]{:S(2)}, u32[]{:S(2)}) collective-permute-start(f32[3,2,256,256]{3,2,1,0:T(8,128)S(1)} %fusion.92), channel_id=1, source_target_pairs={{0,16},{4,20},{8,24},{12,28},{16,0},{20,4},{24,8},{28,12},{1,17},{... | collective-permute-start | bytes 4718600 | tf_op jit(solution)/shard_map/ppermute | solution.py:46
  95.1 1.7 fusion.34
  96.9 2.3 %copy.82 = bf16[1024,512]{0,1:T(8,128)(2,1)} copy(bf16[1024,512]{1,0:T(8,128)(2,1)} %param.8) | data formatting | bytes 2097152 | tf_op jit(solution)/shard_map/reshape | solution.py:65
  99.2 1.0 copy.79
  100.2 0.0 collective-permute-done
  100.2 2.2 %pad_maximum_fusion.3 = bf16[1024,512]{1,0:T(8,128)(2,1)} fusion(bf16[1024,512]{1,0:T(8,128)(2,1)} %param.10, bf16[512,512]{1,0:T(8,128)(2,1)} %collective-permute-done), kind=kLoop, calls=%fused_computation.65 | loop fusion | flops 2097152 | bytes 2621440 | tf_op jit(solution)/shard_map/concatenate | solution.py:61
  102.5 2.3 %copy.34 = bf16[1024,512]{0,1:T(8,128)(2,1)} copy(bf16[1024,512]{1,0:T(8,128)(2,1)} %pad_maximum_fusion.3) | data formatting | bytes 2097152 | tf_op jit(solution)/shard_map/slice | solution.py:75
  104.8 0.0 collective-permute-done.1
  104.8 2.1 %pad_maximum_fusion.2 = bf16[1024,512]{0,1:T(8,128)(2,1)} fusion(bf16[1024,512]{0,1:T(8,128)(2,1)S(1)} %copy.35, bf16[512,512]{0,1:T(8,128)(2,1)} %collective-permute-done.1), kind=kLoop, calls=%fused_computation.64 | loop fusion | flops 2097152 | bytes 2621440 | tf_op jit(solution)/shard_map/concatenate | solution.py:60
  106.9 5.1 %fusion.66 = (f32[2,512]{1,0:T(2,128)S(1)}, f32[2,512,1024]{1,2,0:T(8,128)}) fusion(pred[512,1024]{0,1:T(8,128)(4,1)S(1)} %copy-done.17, bf16[1024,2,256]{0,2,1:T(8,128)(2,1)} %bitcast.169, bf16[512,2,256]{0,2,1:T(8,128)(2,1)} %bitcast.171), kind=kOutput, calls=%fused_computation.95 | convolution fusion | flops 541066240 | bytes 6295552 | tf_op jit(solution)/shard_map/sub | solution.py:86
  112.0 4.4 %fusion.35 = f32[512,2,256]{0,2,1:T(8,128)} fusion(bf16[1024,2,256]{0,2,1:T(8,128)(2,1)} %bitcast.168, f32[2,512,1024]{1,2,0:T(8,128)} %get-tuple-element.24, f32[2,512]{1,0:T(2,128)S(1)} %get-tuple-element.23), kind=kOutput, calls=%fused_computation.57 | convolution fusion | flops 538968064 | bytes 6295552 | tf_op jit(solution)/shard_map/hij,jhd->ihd/dot_general | solution.py:89
  116.4 45.5 %collective-permute-done.4 = f32[3,2,256,256]{3,2,1,0:T(8,128)} collective-permute-done((f32[3,2,256,256]{3,2,1,0:T(8,128)S(1)}, f32[3,2,256,256]{3,2,1,0:T(8,128)}, u32[]{:S(2)}, u32[]{:S(2)}) %collective-permute-start.4) | collective-permute-done | bytes 1572896 | tf_op jit(solution)/shard_map/ppermute | solution.py:46
  162.0 1.8 multiply_reduce_fusion.2
  163.8 1.8 broadcast_multiply_fusion
  165.6 0.1 slice_bitcast_fusion.1
  165.7 0.0 copy-start.13
  165.7 0.0 copy-start.14
  165.7 0.0 copy-start.18
  165.7 1.5 copy-done
  167.2 1.2 fusion.70
  168.5 0.0 copy-start.20
  168.5 1.2 fusion.69
  169.8 5.3 %multiply_reduce_fusion = (f32[1024]{0:T(1024)S(1)}, f32[2,256,1024]{2,1,0:T(8,128)}) fusion(f32[2]{0:T(128)S(1)} %copy-done.20, f32[2,256,256]{2,1,0:T(8,128)S(1)} %get-tuple-element.16, f32[2,256,1024]{1,2,0:T(8,128)S(1)} %fusion.70, f32[2,256,1024]{1,2,0:T(8,128)S(1)} %fusion.69), kind=kOutput, calls=%fused_computation.34 | convolution fusion | flops 1614806016 | bytes 6819848 | tf_op jit(solution)/shard_map/thi,hij->thj/dot_general | solution.py:51
  175.1 5.6 %psum.7 = f32[1024]{0:T(1024)S(1)} all-reduce(f32[1024]{0:T(1024)S(1)} %get-tuple-element.25), channel_id=1, replica_groups=mesh['seq'=8,'head'=4] {'head'}, use_global_device_ids=true, to_apply=%region_7.8 | all-reduce | flops 1024 | bytes 8192 | tf_op jit(solution)/shard_map/psum | solution.py:54
  180.7 2.5 %maximum_add_fusion = f32[1024,2,256]{0,2,1:T(8,128)S(1)} fusion(f32[512,2,256]{0,2,1:T(8,128)S(1)} %copy-done.16, f32[512,2,256]{0,2,1:T(8,128)} %fusion.35, f32[2,256,1024]{2,1,0:T(8,128)} %get-tuple-element.26, f32[1024]{0:T(1024)S(1)} %add_sqrt_fusion, f32[2]{0:T(128)S(1)} %copy-done.20), kind=kLoop, calls=%fused_computation.10 | loop fusion | flops 2097152 | bytes 6295560 | tf_op jit(solution)/shard_map/add | solution.py:92
  183.2 1.8 copy.62
  (27 shorter events, 0.1 us)
Async XLA Ops:
  0.6 1.6 copy-start.8
  2.2 1.3 copy-start.10
  3.5 1.3 copy-start.1
  3.5 1.3 copy-start.6
  3.5 1.3 copy-start.19
  12.8 39.7 %copy-start.4 = (f32[1,2,256,256]{3,2,1,0:T(8,128)}, f32[1,2,256,256]{3,2,1,0:T(8,128)S(1)}, u32[]{:S(2)}) copy-start(f32[1,2,256,256]{3,2,1,0:T(8,128)S(1)} %fusion.40) | copy-start | bytes 1572868
  14.9 39.1 %copy-start.5 = (f32[1,2,256,256]{3,2,1,0:T(8,128)}, f32[1,2,256,256]{3,2,1,0:T(8,128)S(1)}, u32[]{:S(2)}) copy-start(f32[1,2,256,256]{3,2,1,0:T(8,128)S(1)} %fusion.36) | copy-start | bytes 1572868
  15.1 37.4 %collective-permute-start.2 = (f32[3,2,256,256]{3,2,1,0:T(8,128)S(1)}, f32[3,2,256,256]{3,2,1,0:T(8,128)S(1)}, u32[]{:S(2)}, u32[]{:S(2)}) collective-permute-start(f32[3,2,256,256]{3,2,1,0:T(8,128)S(1)} %pad_maximum_fusion.1), channel_id=1, source_target_pairs={{0,4},{4,0},{8,12},{12,8},{16,20},{20,16},{24,28},{28,24},{1,5},{5... | collective-permute-start | bytes 4718600 | tf_op jit(solution)/shard_map/ppermute | solution.py:46
  52.5 1.7 copy-start.3
  54.2 9.9 %copy-start.12 = (bf16[1024,512]{1,0:T(8,128)(2,1)S(1)}, bf16[1024,512]{1,0:T(8,128)(2,1)}, u32[]{:S(2)}) copy-start(bf16[1024,512]{1,0:T(8,128)(2,1)} %param.8) | copy-start | bytes 3145732
  54.2 35.9 %collective-permute-start.3 = (f32[3,2,256,256]{3,2,1,0:T(8,128)}, f32[3,2,256,256]{3,2,1,0:T(8,128)}, u32[]{:S(2)}, u32[]{:S(2)}) collective-permute-start(f32[3,2,256,256]{3,2,1,0:T(8,128)} %fusion.63), channel_id=1, source_target_pairs={{0,8},{4,12},{8,0},{12,4},{16,24},{20,28},{24,16},{28,20},{1,9},{5... | collective-permute-start | bytes 4718600 | tf_op jit(solution)/shard_map/ppermute | solution.py:46
  56.8 43.4 %collective-permute-start = (bf16[512,512]{1,0:T(8,128)(2,1)}, bf16[512,512]{1,0:T(8,128)(2,1)}, u32[]{:S(2)}, u32[]{:S(2)}) collective-permute-start(bf16[512,512]{1,0:T(8,128)(2,1)} %slice.36), channel_id=1, source_target_pairs={{0,4},{4,8},{8,12},{12,16},{16,20},{20,24},{24,28},{1,5},{5,9},{9,... | collective-permute-start | bytes 1572872 | tf_op jit(solution)/shard_map/ppermute | solution.py:14
  61.9 42.9 %collective-permute-start.1 = (bf16[512,512]{0,1:T(8,128)(2,1)}, bf16[512,512]{0,1:T(8,128)(2,1)}, u32[]{:S(2)}, u32[]{:S(2)}) collective-permute-start(bf16[512,512]{0,1:T(8,128)(2,1)} %slice.47), channel_id=1, source_target_pairs={{0,4},{4,8},{8,12},{12,16},{16,20},{20,24},{24,28},{1,5},{5,9},{9,... | collective-permute-start | bytes 1572872 | tf_op jit(solution)/shard_map/ppermute | solution.py:14
  70.6 24.5 %copy-start.2 = (bf16[1024,512]{1,0:T(8,128)(2,1)S(1)}, bf16[1024,512]{1,0:T(8,128)(2,1)}, u32[]{:S(2)}) copy-start(bf16[1024,512]{1,0:T(8,128)(2,1)} %param.10) | copy-start | bytes 3145732
  70.6 24.5 %copy-start.21 = (f32[2,512,1024]{1,2,0:T(8,128)S(1)}, f32[2,512,1024]{1,2,0:T(8,128)}, u32[]{:S(2)}) copy-start(f32[2,512,1024]{1,2,0:T(8,128)} %get-tuple-element.22) | copy-start | bytes 12582916
  92.5 69.5 %collective-permute-start.4 = (f32[3,2,256,256]{3,2,1,0:T(8,128)S(1)}, f32[3,2,256,256]{3,2,1,0:T(8,128)}, u32[]{:S(2)}, u32[]{:S(2)}) collective-permute-start(f32[3,2,256,256]{3,2,1,0:T(8,128)S(1)} %fusion.92), channel_id=1, source_target_pairs={{0,16},{4,20},{8,24},{12,28},{16,0},{20,4},{24,8},{28,12},{1,17},{... | collective-permute-start | bytes 4718600 | tf_op jit(solution)/shard_map/ppermute | solution.py:46
  96.9 2.3 %copy-start.15 = (bf16[512,512]{1,0:T(8,128)(2,1)S(1)}, bf16[512,512]{1,0:T(8,128)(2,1)}, u32[]{:S(2)}) copy-start(bf16[512,512]{1,0:T(8,128)(2,1)} %get-tuple-element.17) | copy-start | bytes 1572868
  102.5 4.5 %copy-start.17 = (pred[512,1024]{0,1:T(8,128)(4,1)S(1)}, pred[512,1024]{0,1:T(8,128)(4,1)}, u32[]{:S(2)}) copy-start(pred[512,1024]{0,1:T(8,128)(4,1)} %get-tuple-element.19) | copy-start | bytes 1572868
  112.0 50.0 %copy-start.7 = (f32[2,256,256]{2,1,0:T(8,128)S(1)}, f32[2,256,256]{2,1,0:T(8,128)}, u32[]{:S(2)}) copy-start(f32[2,256,256]{2,1,0:T(8,128)} %param.15) | copy-start | bytes 1572868
  112.0 50.0 %copy-start.9 = (f32[2,256,256]{2,1,0:T(8,128)S(1)}, f32[2,256,256]{2,1,0:T(8,128)}, u32[]{:S(2)}) copy-start(f32[2,256,256]{2,1,0:T(8,128)} %param.14) | copy-start | bytes 1572868
  112.0 50.0 %copy-start.11 = (f32[2,256,256]{2,1,0:T(8,128)S(1)}, f32[2,256,256]{2,1,0:T(8,128)}, u32[]{:S(2)}) copy-start(f32[2,256,256]{2,1,0:T(8,128)} %param.13) | copy-start | bytes 1572868
  165.6 1.7 copy-start
  165.7 4.1 %copy-start.13 = (f32[2,256,256]{2,1,0:T(8,128)}, f32[2,256,256]{2,1,0:T(8,128)S(1)}, u32[]{:S(2)}) copy-start(f32[2,256,256]{2,1,0:T(8,128)S(1)} %get-tuple-element.14) | copy-start | bytes 1572868
  165.7 4.1 %copy-start.14 = (f32[2,256,256]{2,1,0:T(8,128)}, f32[2,256,256]{2,1,0:T(8,128)S(1)}, u32[]{:S(2)}) copy-start(f32[2,256,256]{2,1,0:T(8,128)S(1)} %get-tuple-element.15) | copy-start | bytes 1572868
  165.7 4.1 %copy-start.18 = (f32[2,256,256]{2,1,0:T(8,128)}, f32[2,256,256]{2,1,0:T(8,128)S(1)}, u32[]{:S(2)}) copy-start(f32[2,256,256]{2,1,0:T(8,128)S(1)} %get-tuple-element.16) | copy-start | bytes 1572868
  168.5 1.3 copy-start.20
  169.8 10.9 %copy-start.16 = (f32[512,2,256]{0,2,1:T(8,128)S(1)}, f32[512,2,256]{0,2,1:T(8,128)}, u32[]{:S(2)}) copy-start(f32[512,2,256]{0,2,1:T(8,128)} %fusion.34) | copy-start | bytes 3145732
